TPU v7x, 32 devices: a whole 2x2x4 slice. The times are simulated.
32 devices in a mesh: rep: 4 (over y, core), fsdp: 8 (over z, x).
Axes of the slice: x: 2, y: 2, z: 4, core: 2. Of those that a mesh axis runs over, the one named last changes fastest.
Arguments:
- activations: bfloat16 [4, 3072, 4096], P('rep', 'fsdp'), may hold values from -6 to 6
- key_cotangent: bfloat16 [4, 3072, 512], P('rep', 'fsdp'), may hold values from -12 to 12
- doc_ids: int32 [4, 3072], P('rep', 'fsdp'), may hold values from 0 to 7, as said below
- replica_params: float32 [4, 4096, 512], P('rep', 'fsdp'), may hold values from -14 to 14
- first_moment: float32 [4, 4096, 512], P('rep', 'fsdp'), may hold values from -6 to 6
- second_moment: float32 [4, 4096, 512], P('rep', 'fsdp'), may hold values from 1 to 16
- anchor: float32 [4096, 512], P(('fsdp', 'rep')), may hold values from -8 to 8
- momentum: float32 [4096, 512], P(('fsdp', 'rep')), may hold values from -3 to 3
Outputs:
- new_first: float32 [4, 4096, 512], P('rep', 'fsdp')
- new_second: float32 [4, 4096, 512], P('rep', 'fsdp')
- new_momentum: float32 [4096, 512], P(('fsdp', 'rep'))
- new_params: float32 [4096, 512], P('fsdp')
Inputs may be any that keep to these rules, and one draw needn't show every extreme that they name: `doc_ids`: within each group the numbers never fall along the tokens; every block of 384 consecutive tokens (from token 0) holds the first token of exactly one document; every document holds 1 to 767 tokens and one holds exactly 767.
All inputs are finite; a program needn't handle non-finite values.
Results may differ from a plain program's by a relative error of at most 0.0035.
Values may be sent and summed in bfloat16 or wider, within the bound.
No kernel may reach another device: no remote copies, remote signals or barrier semaphores. Data moves between devices by JAX's collectives and lax.ppermute only.
A program may use at most 64 MiB of HBM per device.

v0:
```python
import math
import jax
import jax.numpy as jnp
from jax import lax
from jax.sharding import PartitionSpec as P

KV_HEADS = 4
HEAD = 128
rope_base = 500000.0


def entering(array, axis, combine, identity):
    peers, index = (lax.axis_size(axis), lax.axis_index(axis))
    everything = jax.tree.map(lambda part: lax.all_gather(part, axis), array)
    start = jax.tree.map(
        lambda part, zero: jnp.broadcast_to(jnp.asarray(zero, part.dtype), part.shape),
        array,
        identity,
    )

    def hop(k, before):
        reached = k < index
        new = combine(before, jax.tree.map(lambda part: part[k], everything))
        return jax.tree.map(lambda a, b: jnp.where(reached, a, b), new, before)

    return lax.fori_loop(0, peers, hop, start)


def rotate_back(cotangent, offsets):
    row_count = cotangent.shape[0]
    half_head = HEAD // 2
    blocks = cotangent.astype(jnp.float32).reshape(row_count, KV_HEADS, 2, half_head)
    frequency = jnp.exp(
        jnp.arange(half_head, dtype=jnp.float32) * (-math.log(rope_base) / half_head)
    )
    angles = offsets[:, None] * frequency[None, :]
    cosine = jnp.cos(angles)[:, None, :]
    sine_part = jnp.sin(angles)[:, None, :]
    lower_half = blocks[:, :, 0, :]
    upper_half = blocks[:, :, 1, :]
    fresh_lower = lower_half * cosine + upper_half * sine_part
    fresh_upper = upper_half * cosine - lower_half * sine_part
    return (
        jnp.stack([fresh_lower, fresh_upper], axis=2)
        .reshape(row_count, KV_HEADS * HEAD)
        .astype(jnp.bfloat16)
    )


def inner_step(grad, params, first, second):
    fresh_first = 0.9 * first + 0.1 * grad
    fresh_second = 0.95 * second + 0.05 * grad * grad
    stepped = params - 0.2 * (fresh_first / (jnp.sqrt(fresh_second) + 1e-08) + 0.1 * params)
    return (fresh_first, fresh_second, stepped)


def join_runs(before, behind):
    joined_doc = jnp.where(behind[0] < 0, before[0], behind[0])
    joined_start = jnp.where(
        behind[0] < 0, before[1], jnp.where(behind[0] == before[0], before[1], behind[1])
    )
    return (joined_doc, joined_start)


def local(
    activations,
    key_cotangent,
    doc_ids,
    replica_params,
    first_moment,
    second_moment,
    anchor,
    momentum,
):
    features = activations[0]
    cotangent = key_cotangent[0]
    doc_block = doc_ids[0]
    tok_rows = features.shape[0]
    groups = lax.axis_size("fsdp")
    replicas = lax.axis_size("rep")
    device = lax.axis_index("fsdp")
    root = device * tok_rows
    places = jnp.arange(tok_rows, dtype=jnp.int32)
    last_doc = doc_block[tok_rows - 1]
    last_start = jnp.min(jnp.where(doc_block == last_doc, places, jnp.int32(tok_rows))) + root
    prior_doc, prior_start = entering(
        (last_doc, last_start), "fsdp", join_runs, (jnp.int32(-1), jnp.int32(0))
    )
    begins = jnp.concatenate([jnp.ones((1,), jnp.bool_), doc_block[1:] != doc_block[:-1]])
    local_start = lax.cummax(jnp.where(begins, places, jnp.int32(0)), axis=0) + root
    run_start = jnp.where(doc_block == prior_doc, prior_start, local_start)
    offsets = (root + places - run_start).astype(jnp.float32)
    rotated = rotate_back(cotangent, offsets)
    grad_scale = 1.0 / math.sqrt(tok_rows * groups)
    product = lax.dot_general(
        features, rotated, (((0,), (0,)), ((), ())), preferred_element_type=jnp.float32
    )
    grad = lax.psum_scatter(
        (product * grad_scale).astype(jnp.bfloat16), "fsdp", scatter_dimension=0, tiled=True
    ).astype(jnp.float32)
    fresh_first, fresh_second, stepped = inner_step(
        grad, replica_params[0], first_moment[0], second_moment[0]
    )
    share_rows = anchor.shape[0]
    summed = lax.psum(stepped, "rep")
    anchor_rows, momentum_rows = (
        lax.all_gather(anchor, "rep", axis=0, tiled=True),
        lax.all_gather(momentum, "rep", axis=0, tiled=True),
    )
    pseudo_grad = anchor_rows - summed / replicas
    momentum_full = 0.9 * momentum_rows + pseudo_grad
    new_params = anchor_rows - 0.7 * (pseudo_grad + 0.9 * momentum_full)
    new_momentum = lax.dynamic_slice_in_dim(
        momentum_full, lax.axis_index("rep") * share_rows, share_rows, 0
    )
    return (fresh_first[None], fresh_second[None], new_momentum, new_params)


def solution(mesh):
    placed = (
        P("rep", "fsdp", None),
        P("rep", "fsdp", None),
        P("rep", "fsdp"),
        P("rep", "fsdp", None),
        P("rep", "fsdp", None),
        P("rep", "fsdp", None),
        P(("fsdp", "rep"), None),
        P(("fsdp", "rep"), None),
    )
    return jax.shard_map(
        local,
        mesh=mesh,
        in_specs=placed,
        out_specs=(
            P("rep", "fsdp", None),
            P("rep", "fsdp", None),
            P(("fsdp", "rep"), None),
            P("fsdp", None),
        ),
        check_vma=False,
    )
```

profile of v0, /device:TPU:0, one launch (start us, length us, event | category | flops | bytes accessed | tf_op | source)
XLA Modules:
  0.0 208.1 jit_solution(2617310549342385104)
XLA Ops:
  8.1 1.4 slice.28
  9.5 0.8 compare_reduce_fusion
  10.3 1.2 copy.22
  11.5 0.9 convert.9
  12.5 1.3 compare_reduce_fusion.2
  13.7 0.7 select_reduce_fusion
  14.4 1.2 dynamic-slice
  15.6 1.2 bitcast_dynamic-update-slice_fusion
  17.5 0.8 dynamic-update-slice.1
  18.3 13.1 %all-reduce.2 = (s32[8]{0:T(128)S(1)}, s32[8]{0:T(128)S(1)}) all-reduce(s32[8]{0:T(128)S(1)} %bitcast_dynamic-update-slice_fusion, s32[8]{0:T(128)S(1)} %dynamic-update-slice.1), channel_id=2, replica_groups=mesh['rep'=4,'fsdp'=8] {'fsdp'}, use_global_device_ids=true, to_apply=%add | all-reduce | flops 16 | bytes 128 | tf_op jit(solution)/shard_map/all_gather | solution.py:14
  31.3 27.6 %while.15 = (s32[]{:T(128)}, s32[]{:T(128)}, s32[]{:T(128)}, s32[]{:T(128)}, s32[8]{0:T(128)S(1)}, /*index=5*/s32[8]{0:T(128)S(1)}, s32[]{:T(128)}, s32[]{:T(128)}) while((s32[]{:T(128)}, s32[]{:T(128)}, s32[]{:T(128)}, s32[]{:T(128)}, s32[8]{0:T(128)S(1)}, /*index=5*/s32[8]{0:T(128)S(1)}, s32[]{:T(128)}, s32[]{:T(128)}) %tuple.39), condition=%wide.region_2.3_spmd, body=%wide.region_1.2_spmd.sunk | while | flops 10 | bytes 217 | solution.py:26
  31.3 0.6 dynamic_slice.21
  33.6 0.6 dynamic_slice.22
  34.8 0.6 dynamic_slice.21
  37.0 0.6 dynamic_slice.22
  38.2 0.6 dynamic_slice.21
  40.5 0.6 dynamic_slice.22
  41.7 0.6 dynamic_slice.21
  43.9 0.6 dynamic_slice.22
  45.1 0.6 dynamic_slice.21
  47.4 0.6 dynamic_slice.22
  48.6 0.6 dynamic_slice.21
  50.8 0.6 dynamic_slice.22
  52.0 0.6 dynamic_slice.21
  54.3 0.6 dynamic_slice.22
  55.5 0.6 dynamic_slice.21
  57.7 0.6 dynamic_slice.22
  58.9 0.7 compare_reduce_fusion.1
  59.7 0.3 reduce-window.9
  60.1 0.1 slice_reduce_fusion
  60.2 0.1 fusion.9
  60.3 0.4 multiply_cosine_fusion
  60.7 1.2 add_convert_fusion
  62.0 4.3 %fusion = bf16[4096,512]{0,1:T(8,128)(2,1)} fusion(bf16[384,512]{0,1:T(8,128)(2,1)S(1)} %bitcast.56, bf16[1,384,4096]{2,1,0:T(8,128)(2,1)S(1)} %copy-done), kind=kOutput, calls=%fused_computation.1 | convolution fusion | flops 1614807040 | bytes 7733248 | tf_op jit(solution)/shard_map/dot_general | solution.py:95
  66.4 0.9 copy-done.1
  67.3 0.8 copy.25
  68.2 1.8 copy.24
  70.1 2.5 %copy.26 = f32[1,512,512]{1,2,0:T(8,128)} copy(f32[1,512,512]{2,1,0:T(8,128)} %param.13) | data formatting | bytes 2097152 | tf_op args[3]
  72.6 2.6 %copy.21 = f32[1,512,512]{1,2,0:T(8,128)} copy(f32[1,512,512]{2,1,0:T(8,128)} %param.14) | data formatting | bytes 2097152 | tf_op args[4]
  75.2 2.5 %copy.23 = f32[1,512,512]{1,2,0:T(8,128)} copy(f32[1,512,512]{2,1,0:T(8,128)} %param.15) | data formatting | bytes 2097152 | tf_op args[5]
  77.7 75.5 %reduce-scatter.2.cloned.1.call-done = bf16[512,512]{0,1:T(8,128)(2,1)} async-done(((bf16[4096,512]{0,1:T(8,128)(2,1)}), bf16[512,512]{0,1:T(8,128)(2,1)}) %reduce-scatter.2.cloned.1.call-update) | async-done | bytes 524304 | tf_op jit(solution)/shard_map/reduce_scatter | solution.py:98
  153.2 4.1 %bitcast_subtract_fusion = (f32[512,512]{0,1:T(8,128)}, f32[1,512,512]{1,2,0:T(8,128)}, f32[1,512,512]{1,2,0:T(8,128)}) fusion(f32[1,512,512]{1,2,0:T(8,128)} %copy.26, bf16[512,512]{0,1:T(8,128)(2,1)} %reduce-scatter.2.cloned.1.call-done, f32[1,512,512]{1,2,0:T(8,128)} %copy.21, f32[1,512,512]{1,2,0:T(8,128)} %copy.23), kind=kLoop, calls=%fused_computation.7 | loop fusion | flops 3670016 | bytes 6815744 | tf_op jit(solution)/shard_map/sub | solution.py:53
  157.4 2.5 %copy.27 = f32[1,512,512]{2,1,0:T(8,128)} copy(f32[1,512,512]{1,2,0:T(8,128)} %get-tuple-element.142) | data formatting | bytes 2097152
  159.9 2.5 %copy.28 = f32[1,512,512]{2,1,0:T(8,128)} copy(f32[1,512,512]{1,2,0:T(8,128)} %get-tuple-element.141) | data formatting | bytes 2097152
  162.4 31.4 %all-reduce.5.cloned.1.call-done = f32[512,512]{0,1:T(8,128)} async-done(((f32[512,512]{0,1:T(8,128)}), f32[512,512]{0,1:T(8,128)}) %all-reduce.5.cloned.1.call-update) | async-done | bytes 1048592 | tf_op jit(solution)/shard_map/psum | solution.py:105
  193.8 3.3 %multiply_subtract_fusion = (f32[512,512]{0,1:T(8,128)}, f32[512,512]{0,1:T(8,128)S(1)}) fusion(f32[512,512]{0,1:T(8,128)} %all-gather.6.cloned.1.call-done, f32[512,512]{0,1:T(8,128)} %all-reduce.5.cloned.1.call-done, f32[512,512]{0,1:T(8,128)} %all-gather.4.cloned.1.call-done), kind=kLoop, calls=%fused_computation.11 | loop fusion | flops 2097152 | bytes 5242880 | tf_op jit(solution)/shard_map/sub | solution.py:112
  197.2 0.8 copy.29
  198.0 2.5 %copy.30 = f32[512,512]{1,0:T(8,128)} copy(f32[512,512]{0,1:T(8,128)} %get-tuple-element.138) | data formatting | bytes 2097152
  (21 shorter events, 0.5 us)
Async XLA Ops:
  8.0 54.0 %copy-start = (bf16[1,384,4096]{2,1,0:T(8,128)(2,1)S(1)}, bf16[1,384,4096]{2,1,0:T(8,128)(2,1)}, u32[]{:S(2)}) copy-start(bf16[1,384,4096]{2,1,0:T(8,128)(2,1)} %param.10) | copy-start | bytes 9437188
  8.0 145.2 %reduce-scatter.2.cloned.1.call-start = ((), (), s32[]{:S(2)}) async-start(), calls=%async_computation.1 | async-start | bytes 4718592 | tf_op jit(solution)/shard_map/reduce_scatter | solution.py:98
  66.3 0.9 copy-start.1
  66.3 96.1 %all-gather.6.cloned.1.call-start = ((), (), s32[]{:S(2)}) async-start(), calls=%async_computation.3 | async-start | bytes 1310720 | tf_op jit(solution)/shard_map/all_gather | solution.py:107
  68.1 94.3 %all-gather.4.cloned.1.call-start = ((), (), s32[]{:S(2)}) async-start(), calls=%async_computation.2 | async-start | bytes 1310720 | tf_op jit(solution)/shard_map/all_gather | solution.py:108
  70.0 123.8 %all-reduce.5.cloned.1.call-start = ((), (), s32[]{:S(2)}) async-start(), calls=%async_computation.4 | async-start | bytes 2097152 | tf_op jit(solution)/shard_map/psum | solution.py:105
Sparse Core Ops, SparseCore 0:
  66.5 86.6 reduce-scatter.1
Sparse Core Ops, SparseCore 1:
  69.0 14.9 all-gather.5
  85.5 16.7 all-gather.3
  157.4 36.4 all-reduce.4
where the time goes:
time: 209 us; the launch traced here: 208 us
  waiting for transfers between devices  107 us (51%)
  local copies, waits for them, and re-layouts  34.9 us (17%)
  loops' own time  18.3 us (9%)
  between operations  16.4 us (8%)
  other arithmetic  14 us (7%)
  blocking collectives  13.1 us (6%)
  matrix products  4.28 us (2%)
    reduce_scatter x1, waiting for transfers between devices, local(): lax.psum_scatter((product * grad_scale).astype(jnp.bfloat16), 'fsdp', sca...  75.5 us
    psum x1, waiting for transfers between devices, local(): summed = lax.psum(stepped, 'rep')  31.4 us
    unnamed x19, local copies, waits for them, and re-layouts  24 us
    another operation x1, loops' own time, entering(): return lax.fori_loop(0, peers, hop, start)  18.3 us
    all_gather x1, blocking collectives, entering(): everything = jax.tree.map(lambda part: lax.all_gather(part, axis), array)  13.1 us
    dynamic_slice x16, local copies, waits for them, and re-layouts, hop(): new = combine(before, jax.tree.map(lambda part: part[k], everything))  9.29 us
    dot_general x1, matrix products, local(): lax.dot_general(features, rotated, (((0,), (0,)), ((), ())), preferred_el...  4.28 us
  transfers between devices with their start and end apart: 4, of which 2 were waited for; matrix products, arithmetic and copies ran while one was open for 9% of the time, Pallas kernels for 0%

commit v1 on v0

--- a/solution.py
+++ b/solution.py
@@ -102,7 +102,7 @@
         grad, replica_params[0], first_moment[0], second_moment[0]
     )
     share_rows = anchor.shape[0]
-    summed = lax.psum(stepped, "rep")
+    summed = lax.all_gather(stepped, "rep").sum(axis=0)
     anchor_rows, momentum_rows = (
         lax.all_gather(anchor, "rep", axis=0, tiled=True),
         lax.all_gather(momentum, "rep", axis=0, tiled=True),

time: 209 us -> 246 us (1.18)
  waiting for transfers between devices: 107 us -> 131 us
  local copies, waits for them, and re-layouts: 34.9 us -> 42 us
  other arithmetic: 14 us -> 18.2 us
  loops' own time: 18.3 us -> 21.3 us
    psum x1 -> x0, waiting for transfers between devices: 31.4 us -> none  [local(): summed = lax.psum(stepped, 'rep')]
    all_gather x0 -> x1, waiting for transfers between devices: none -> 26.4 us  [local(): summed = lax.all_gather(stepped, 'rep').sum(axis=0)]
    all_gather x1, waiting for transfers between devices: 0.01 us -> 18.9 us  [local(): lax.all_gather(anchor, 'rep', axis=0, tiled=True)]
    all_gather x1, waiting for transfers between devices: 0.01 us -> 6.75 us  [local(): lax.all_gather(momentum, 'rep', axis=0, tiled=True)]
    all_gather x0 -> x1, local copies, waits for them, and re-layouts: none -> 6.02 us  [local(): summed = lax.all_gather(stepped, 'rep').sum(axis=0)]
    reduce_sum x0 -> x1, other arithmetic: none -> 5.74 us  [local(): summed = lax.all_gather(stepped, 'rep').sum(axis=0)]
    reduce_scatter x1, waiting for transfers between devices: 75.5 us -> 79.1 us  [local(): lax.psum_scatter((product * grad_scale).astype(jnp.bfloat16), 'fsdp', sca...]
    another operation x1, loops' own time: 18.3 us -> 21.3 us  [entering(): return lax.fori_loop(0, peers, hop, start)]
  transfers between devices with their start and end apart: 4 -> 4, of which waited for: 2 -> 4; matrix products, arithmetic and copies ran while one was open for 9% -> 11% of each run, Pallas kernels for 0% -> 0%
where the time goes in v1:
time: 246 us; the launch traced here: 245 us
  waiting for transfers between devices  131 us (53%)
  local copies, waits for them, and re-layouts  42 us (17%)
  loops' own time  21.3 us (9%)
  other arithmetic  18.2 us (7%)
  between operations  14.5 us (6%)
  blocking collectives  13.1 us (5%)
  matrix products  4.27 us (2%)
    reduce_scatter x1, waiting for transfers between devices, local(): lax.psum_scatter((product * grad_scale).astype(jnp.bfloat16), 'fsdp', sca...  79.1 us
    all_gather x1, waiting for transfers between devices, local(): summed = lax.all_gather(stepped, 'rep').sum(axis=0)  26.4 us
    unnamed x19, local copies, waits for them, and re-layouts  23.4 us
    another operation x1, loops' own time, entering(): return lax.fori_loop(0, peers, hop, start)  21.3 us
    all_gather x1, waiting for transfers between devices, local(): lax.all_gather(anchor, 'rep', axis=0, tiled=True)  18.9 us
    all_gather x1, blocking collectives, entering(): everything = jax.tree.map(lambda part: lax.all_gather(part, axis), array)  13.1 us
    dynamic_slice x16, local copies, waits for them, and re-layouts, hop(): new = combine(before, jax.tree.map(lambda part: part[k], everything))  9.99 us
    all_gather x1, waiting for transfers between devices, local(): lax.all_gather(momentum, 'rep', axis=0, tiled=True)  6.75 us
  transfers between devices with their start and end apart: 4, of which 4 were waited for; matrix products, arithmetic and copies ran while one was open for 11% of the time, Pallas kernels for 0%

profile of v1, /device:TPU:0, one launch (start us, length us, event | category | flops | bytes accessed | tf_op | source)
XLA Modules:
  0.0 244.9 jit_solution(18047215226848955010)
XLA Ops:
  7.2 1.5 slice.28
  8.7 0.8 compare_reduce_fusion
  9.6 1.4 compare_reduce_fusion.2
  11.0 0.6 select_reduce_fusion
  12.2 1.2 dynamic-slice
  13.5 1.4 bitcast_dynamic-update-slice_fusion
  14.9 0.8 dynamic-update-slice.1
  15.6 13.1 %all-reduce.2 = (s32[8]{0:T(128)S(1)}, s32[8]{0:T(128)S(1)}) all-reduce(s32[8]{0:T(128)S(1)} %bitcast_dynamic-update-slice_fusion, s32[8]{0:T(128)S(1)} %dynamic-update-slice.1), channel_id=2, replica_groups=mesh['rep'=4,'fsdp'=8] {'fsdp'}, use_global_device_ids=true, to_apply=%add | all-reduce | flops 16 | bytes 128 | tf_op jit(solution)/shard_map/all_gather | solution.py:14
  28.7 31.3 %while.15 = (s32[]{:T(128)}, s32[]{:T(128)}, s32[]{:T(128)}, s32[]{:T(128)}, s32[8]{0:T(128)S(1)}, /*index=5*/s32[8]{0:T(128)S(1)}, s32[]{:T(128)}, s32[]{:T(128)}) while((s32[]{:T(128)}, s32[]{:T(128)}, s32[]{:T(128)}, s32[]{:T(128)}, s32[8]{0:T(128)S(1)}, /*index=5*/s32[8]{0:T(128)S(1)}, s32[]{:T(128)}, s32[]{:T(128)}) %tuple.40), condition=%wide.region_2.3_spmd, body=%wide.region_1.2_spmd.sunk | while | flops 10 | bytes 201 | solution.py:26
  28.7 0.7 dynamic_slice.21
  30.0 0.6 dynamic_slice.22
  32.6 0.7 dynamic_slice.21
  34.0 0.6 dynamic_slice.22
  36.5 0.7 dynamic_slice.21
  37.9 0.6 dynamic_slice.22
  40.4 0.7 dynamic_slice.21
  41.8 0.6 dynamic_slice.22
  44.3 0.7 dynamic_slice.21
  45.7 0.6 dynamic_slice.22
  48.2 0.7 dynamic_slice.21
  49.6 0.6 dynamic_slice.22
  52.2 0.7 dynamic_slice.21
  53.5 0.6 dynamic_slice.22
  56.1 0.7 dynamic_slice.21
  57.4 0.6 dynamic_slice.22
  60.0 0.7 compare_reduce_fusion.1
  60.8 0.3 reduce-window.9
  61.3 1.2 copy.24
  62.7 0.4 multiply_cosine_fusion
  63.3 4.3 %fusion = bf16[4096,512]{0,1:T(8,128)(2,1)} fusion(bf16[384,512]{0,1:T(8,128)(2,1)S(1)} %bitcast.58, bf16[1,384,4096]{2,1,0:T(8,128)(2,1)S(1)} %copy-done), kind=kOutput, calls=%fused_computation.1 | convolution fusion | flops 1614807040 | bytes 7733248 | tf_op jit(solution)/shard_map/dot_general | solution.py:95
  67.6 2.5 %copy.23 = f32[1,512,512]{1,2,0:T(8,128)} copy(f32[1,512,512]{2,1,0:T(8,128)} %param.14) | data formatting | bytes 2097152 | tf_op args[4]
  70.1 2.5 %copy.25 = f32[1,512,512]{1,2,0:T(8,128)} copy(f32[1,512,512]{2,1,0:T(8,128)} %param.15) | data formatting | bytes 2097152 | tf_op args[5]
  72.7 2.6 %copy.28 = f32[1,512,512]{1,2,0:T(8,128)} copy(f32[1,512,512]{2,1,0:T(8,128)} %param.13) | data formatting | bytes 2097152 | tf_op args[3]
  75.3 79.1 %reduce-scatter.2.cloned.1.call-done = bf16[512,512]{0,1:T(8,128)(2,1)} async-done(((bf16[4096,512]{0,1:T(8,128)(2,1)}), bf16[512,512]{0,1:T(8,128)(2,1)}) %reduce-scatter.2.cloned.1.call-update) | async-done | bytes 524304 | tf_op jit(solution)/shard_map/reduce_scatter | solution.py:98
  154.4 4.1 %bitcast_subtract_fusion = (f32[512,512]{0,1:T(8,128)}, f32[1,512,512]{1,2,0:T(8,128)}, f32[1,512,512]{1,2,0:T(8,128)}) fusion(f32[1,512,512]{1,2,0:T(8,128)} %copy.28, bf16[512,512]{0,1:T(8,128)(2,1)} %reduce-scatter.2.cloned.1.call-done, f32[1,512,512]{1,2,0:T(8,128)} %copy.23, f32[1,512,512]{1,2,0:T(8,128)} %copy.25), kind=kLoop, calls=%fused_computation.7 | loop fusion | flops 3670016 | bytes 6815744 | tf_op jit(solution)/shard_map/sub | solution.py:53
  158.6 0.9 copy.26
  159.6 1.8 copy.27
  161.4 2.5 %copy.29 = f32[1,512,512]{2,1,0:T(8,128)} copy(f32[1,512,512]{1,2,0:T(8,128)} %get-tuple-element.146) | data formatting | bytes 2097152
  163.9 2.6 %copy.30 = f32[1,512,512]{2,1,0:T(8,128)} copy(f32[1,512,512]{1,2,0:T(8,128)} %get-tuple-element.145) | data formatting | bytes 2097152
  166.5 26.4 %all-gather.10.cloned.1.call-done = f32[2048,512]{0,1:T(8,128)} async-done(((f32[512,512]{0,1:T(8,128)}), f32[2048,512]{0,1:T(8,128)}) %all-gather.10.cloned.1.call-update) | async-done | bytes 4194320 | tf_op jit(solution)/shard_map/all_gather | solution.py:105
  193.0 6.0 %reshape.127 = f32[4,512,512]{1,0,2:T(4,128)} reshape(f32[2048,512]{0,1:T(8,128)} %all-gather.10.cloned.1.call-done) | data formatting | bytes 8388608 | tf_op jit(solution)/shard_map/all_gather | solution.py:105
  199.0 5.7 %reduce_sum.9 = f32[512,512]{0,1:T(8,128)} reduce(f32[4,512,512]{1,0,2:T(4,128)} %reshape.127, f32[]{:T(128)} %constant.66.clone.1), dimensions={0}, to_apply=%region_6.7 | reduce | flops 786432 | bytes 5242884 | tf_op jit(solution)/shard_map/reduce_sum | solution.py:105
  204.7 6.8 %all-gather.6.cloned.1.call-done = f32[512,512]{0,1:T(8,128)} async-done(((f32[128,512]{0,1:T(8,128)}), f32[512,512]{0,1:T(8,128)}) %all-gather.6.cloned.1.call-update) | async-done | bytes 1048592 | tf_op jit(solution)/shard_map/all_gather | solution.py:108
  211.5 18.9 %all-gather.8.cloned.1.call-done = f32[512,512]{0,1:T(8,128)} async-done(((f32[128,512]{0,1:T(8,128)}), f32[512,512]{0,1:T(8,128)}) %all-gather.8.cloned.1.call-update) | async-done | bytes 1048592 | tf_op jit(solution)/shard_map/all_gather | solution.py:107
  230.4 3.6 %multiply_subtract_fusion = (f32[512,512]{0,1:T(8,128)}, f32[512,512]{0,1:T(8,128)}) fusion(f32[512,512]{0,1:T(8,128)} %all-gather.8.cloned.1.call-done, f32[512,512]{0,1:T(8,128)} %reduce_sum.9, f32[512,512]{0,1:T(8,128)} %all-gather.6.cloned.1.call-done), kind=kLoop, calls=%fused_computation.11 | loop fusion | flops 2097152 | bytes 5242880 | tf_op jit(solution)/shard_map/sub | solution.py:112
  234.1 2.5 %copy.32 = f32[512,512]{1,0:T(8,128)} copy(f32[512,512]{0,1:T(8,128)} %get-tuple-element.142) | data formatting | bytes 2097152
  236.6 1.0 constant_dynamic-slice_fusion
  237.6 0.8 copy.31
  (23 shorter events, 0.8 us)
Async XLA Ops:
  7.2 56.1 %copy-start = (bf16[1,384,4096]{2,1,0:T(8,128)(2,1)S(1)}, bf16[1,384,4096]{2,1,0:T(8,128)(2,1)}, u32[]{:S(2)}) copy-start(bf16[1,384,4096]{2,1,0:T(8,128)(2,1)} %param.10) | copy-start | bytes 9437188
  7.2 147.2 %reduce-scatter.2.cloned.1.call-start = ((), (), s32[]{:S(2)}) async-start(), calls=%async_computation.1 | async-start | bytes 4718592 | tf_op jit(solution)/shard_map/reduce_scatter | solution.py:98
  67.6 125.4 %all-gather.10.cloned.1.call-start = ((), (), s32[]{:S(2)}) async-start(), calls=%async_computation.4 | async-start | bytes 5242880 | tf_op jit(solution)/shard_map/all_gather | solution.py:105
  75.3 83.4 %copy-start.1 = (f32[128,512]{1,0:T(8,128)S(1)}, f32[128,512]{1,0:T(8,128)}, u32[]{:S(2)}) copy-start(f32[128,512]{1,0:T(8,128)} %param.17) | copy-start | bytes 786436
  158.6 52.9 %all-gather.6.cloned.1.call-start = ((), (), s32[]{:S(2)}) async-start(), calls=%async_computation.2 | async-start | bytes 1310720 | tf_op jit(solution)/shard_map/all_gather | solution.py:108
  159.5 70.9 %all-gather.8.cloned.1.call-start = ((), (), s32[]{:S(2)}) async-start(), calls=%async_computation.3 | async-start | bytes 1310720 | tf_op jit(solution)/shard_map/all_gather | solution.py:107
Sparse Core Ops, SparseCore 0:
  67.7 86.6 reduce-scatter.1
  158.7 34.2 all-gather.9
  194.6 16.8 all-gather.5
  213.5 16.8 all-gather.7
